TPU v7x, 512 devices: a whole 4x8x8 slice. The times are simulated.
512 devices in a mesh: layer: 32 (over x_lo, y, core), feat: 16 (over z, x_hi).
Axes of the slice: x: 4 (x_hi: 2, x_lo: 2; x = x_hi * 2 + x_lo), y: 8, z: 8, core: 2. Of those that a mesh axis runs over, the one named last changes fastest.
Arguments:
- latents: bfloat16 [2048, 16384], P('layer', 'feat'), may hold values from 0.5 to 3
- block_lists: int32 [4, 16, 64], replicated, may hold values from 0 to 127, all different within a row
- decoders: bfloat16 [2, 16384, 32768], P(None, 'feat', 'layer'), may hold values from -0.03125 to 0.03125
- targets: bfloat16 [512, 32768], P('feat', 'layer'), may hold values from -6 to 6
Outputs:
- errors: bfloat16 [512, 32768], P('feat', 'layer')
- latent_grad: float32 [2048, 16384], P('layer', 'feat')
Inputs may be any that keep to these rules, and one draw needn't show every extreme that they name: `block_lists`: each row names 64 different latent blocks, and every block is named by some row.
All inputs are finite; a program needn't handle non-finite values.
Results may differ from a plain program's by a relative error of at most 0.006.
Values may be sent and summed in bfloat16 or wider, within the bound.
No kernel may reach another device: no remote copies, remote signals or barrier semaphores. Data moves between devices by JAX's collectives and lax.ppermute only.
A program may use at most 64 MiB of HBM per device.

v0:
```python
import jax
import jax.numpy as jnp
from jax import lax
from jax.sharding import PartitionSpec as P

D = 8192
BLOCK = 128


def swapped(value, axis, bit):
    mask = 2**bit
    pairs = [(source, source ^ mask) for source in range(lax.axis_size(axis))]
    return lax.ppermute(value, axis, pairs)


def passed_along(value, axis, steps):
    count = lax.axis_size(axis)
    first, last = (max(0, -steps), min(count, count - steps))
    return lax.ppermute(value, axis, [(source, source + steps) for source in range(first, last)])


def doubled(held_rows, partner_rows, upper_half):
    return jnp.where(
        upper_half,
        jnp.concatenate([partner_rows, held_rows], 0),
        jnp.concatenate([held_rows, partner_rows], 0),
    )


def pick_half(block, upper_half, axis):
    half_rows = block.shape[axis] // 2
    lower = lax.slice_in_dim(block, 0, half_rows, axis=axis)
    higher = lax.slice_in_dim(block, half_rows, 2 * half_rows, axis=axis)
    return (jnp.where(upper_half, higher, lower), jnp.where(upper_half, lower, higher))


def local(latents, block_lists, decoders, targets):
    layer_pos = lax.axis_index("layer")
    feat_pos = lax.axis_index("feat")
    width_cols = decoders.shape[2]
    groups = D // width_cols
    width_bits = groups.bit_length() - 1
    layer_id = layer_pos // groups
    member = layer_pos % groups
    quarter, feat_cols = latents.shape
    total_rows = quarter * groups
    block_rows = total_rows // block_lists.shape[1]
    blocks_here = feat_cols // BLOCK
    lists = lax.dynamic_index_in_dim(block_lists, layer_id, 0, keepdims=False)
    wanted = feat_pos * blocks_here + jnp.arange(blocks_here, dtype=jnp.int32)
    hit = jnp.any(lists[:, :, None] == wanted[None, None, :], axis=1)
    row_hit = jnp.repeat(hit, block_rows, axis=0)
    row_hit = lax.dynamic_slice_in_dim(row_hit, member * quarter, quarter, 0)
    tile_mask = jnp.repeat(row_hit, BLOCK, axis=1)
    own_tile = jnp.where(tile_mask, latents, jnp.zeros_like(latents))
    own_all = own_tile
    for bit_pos in range(width_bits):
        upper_half = member // (1 << bit_pos) % 2 == 1
        partner_rows = swapped(own_all, "layer", bit_pos)
        own_all = doubled(own_all, partner_rows, upper_half)
    prior_all = passed_along(own_all, "layer", groups)
    summed = jnp.dot(own_all, decoders[0], preferred_element_type=jnp.float32)
    recon_rows = lax.psum_scatter(
        summed + jnp.dot(prior_all, decoders[1], preferred_element_type=jnp.float32),
        "feat",
        scatter_dimension=0,
        tiled=True,
    )
    errors_here = (recon_rows - targets.astype(jnp.float32)).astype(jnp.bfloat16)
    grad_terms = jnp.einsum(
        "tc,kfc->ktf",
        lax.all_gather(errors_here, "feat", axis=0, tiled=True),
        decoders,
        preferred_element_type=jnp.float32,
    )
    grad_pair = grad_terms
    for bit_pos in reversed(range(width_bits)):
        upper_half = member // (1 << bit_pos) % 2 == 1
        kept_part, sent_part = pick_half(grad_pair, upper_half, 1)
        grad_pair = kept_part + swapped(sent_part.astype(jnp.bfloat16), "layer", bit_pos).astype(
            sent_part.dtype
        )
    from_next = passed_along(grad_pair[1].astype(jnp.bfloat16), "layer", -groups).astype(
        jnp.float32
    )
    combined = grad_pair[0] + from_next
    latent_grad = jnp.where(tile_mask, combined, jnp.zeros_like(combined))
    return (errors_here, latent_grad)


def solution(mesh):
    placed = (P("layer", "feat"), P(), P(None, "feat", "layer"), P("feat", "layer"))
    return jax.shard_map(
        local,
        mesh=mesh,
        in_specs=placed,
        out_specs=(P("feat", "layer"), P("layer", "feat")),
        check_vma=False,
    )
```

profile of v0, /device:TPU:32, one launch (start us, length us, event | category | flops | bytes accessed | tf_op | source)
XLA Modules:
  0.0 507.5 jit_solution(15915799173783199281)
XLA Ops:
  7.3 0.7 copy-done
  7.9 0.4 compare_reduce_fusion
  8.4 0.1 broadcast_in_dim.15
  8.5 0.9 bitcast_select_fusion
  9.5 1.9 collective-permute-start
  11.4 1.3 collective-permute-done
  12.8 2.6 collective-permute-start.1
  15.4 7.6 %collective-permute-done.1 = bf16[128,1024]{1,0:T(8,128)(2,1)S(1)} collective-permute-done((bf16[128,1024]{1,0:T(8,128)(2,1)S(1)}, bf16[128,1024]{1,0:T(8,128)(2,1)S(1)}, u32[]{:S(2)}, u32[]{:S(2)}) %collective-permute-start.1) | collective-permute-done | bytes 262176 | tf_op jit(solution)/shard_map/ppermute | solution.py:13
  23.0 0.1 maximum_select_fusion.1
  23.2 2.7 collective-permute-start.2
  25.9 24.4 %collective-permute-done.2 = bf16[256,1024]{1,0:T(8,128)(2,1)S(1)} collective-permute-done((bf16[256,1024]{1,0:T(8,128)(2,1)S(1)}, bf16[256,1024]{1,0:T(8,128)(2,1)S(1)}, u32[]{:S(2)}, u32[]{:S(2)}) %collective-permute-start.2) | collective-permute-done | bytes 524320 | tf_op jit(solution)/shard_map/ppermute | solution.py:13
  50.3 0.5 maximum_select_fusion
  50.8 3.2 collective-permute-start.3
  54.0 47.8 %collective-permute-done.3 = bf16[512,1024]{1,0:T(8,128)(2,1)S(1)} collective-permute-done((bf16[512,1024]{1,0:T(8,128)(2,1)S(1)}, bf16[512,1024]{1,0:T(8,128)(2,1)S(1)}, u32[]{:S(2)}, u32[]{:S(2)}) %collective-permute-start.3) | collective-permute-done | bytes 1048608 | tf_op jit(solution)/shard_map/ppermute | solution.py:19
  101.9 2.9 fusion
  104.7 2.6 fusion.6
  107.4 219.6 %reduce-scatter.2.cloned.1.call-done = f32[32,1024]{1,0:T(8,128)} async-done(((f32[512,1024]{1,0:T(8,128)}), f32[32,1024]{1,0:T(8,128)}) %reduce-scatter.2.cloned.1.call-update) | async-done | bytes 131088 | tf_op jit(solution)/shard_map/reduce_scatter | solution.py:63
  327.0 1.5 subtract_convert_fusion
  328.6 84.4 %all-gather.2.cloned.1.call-done = bf16[512,1024]{1,0:T(8,128)(2,1)} async-done(((bf16[32,1024]{1,0:T(8,128)(2,1)}), bf16[512,1024]{1,0:T(8,128)(2,1)}) %all-gather.2.cloned.1.call-update) | async-done | bytes 1048592 | tf_op jit(solution)/shard_map/all_gather | solution.py:72
  413.0 4.9 convolution_bitcast_fusion
  417.9 0.2 select_convert_fusion
  418.1 2.5 collective-permute-start.4
  420.6 44.0 %collective-permute-done.4 = bf16[2,256,1024]{2,1,0:T(8,128)(2,1)S(1)} collective-permute-done((bf16[2,256,1024]{2,1,0:T(8,128)(2,1)S(1)}, bf16[2,256,1024]{2,1,0:T(8,128)(2,1)S(1)}, u32[]{:S(2)}, u32[]{:S(2)}) %collective-permute-start.4) | collective-permute-done | bytes 1048608 | tf_op jit(solution)/shard_map/ppermute | solution.py:13
  464.6 0.6 convert_add_fusion
  465.4 1.9 collective-permute-start.5
  467.3 13.8 %collective-permute-done.5 = bf16[2,128,1024]{2,1,0:T(8,128)(2,1)S(1)} collective-permute-done((bf16[2,128,1024]{2,1,0:T(8,128)(2,1)S(1)}, bf16[2,128,1024]{2,1,0:T(8,128)(2,1)S(1)}, u32[]{:S(2)}, u32[]{:S(2)}) %collective-permute-start.5) | collective-permute-done | bytes 524320 | tf_op jit(solution)/shard_map/ppermute | solution.py:13
  481.1 0.3 convert_add_fusion.1
  481.4 1.9 collective-permute-start.6
  483.3 1.5 collective-permute-done.6
  485.0 1.9 collective-permute-start.7
  486.9 13.0 %collective-permute-done.7 = bf16[64,1024]{1,0:T(8,128)(2,1)S(1)} collective-permute-done((bf16[64,1024]{1,0:T(8,128)(2,1)S(1)}, bf16[64,1024]{1,0:T(8,128)(2,1)S(1)}, u32[]{:S(2)}, u32[]{:S(2)}) %collective-permute-start.7) | collective-permute-done | bytes 131104 | tf_op jit(solution)/shard_map/ppermute | solution.py:19
  499.9 0.8 fusion.11
  (18 shorter events, 0.5 us)
Async XLA Ops:
  7.2 0.8 copy-start
  7.2 319.8 %reduce-scatter.2.cloned.1.call-start = ((), (), s32[]{:S(2)}) async-start(), calls=%async_computation.1 | async-start | bytes 2228224 | tf_op jit(solution)/shard_map/reduce_scatter | solution.py:63
  9.5 3.2 collective-permute-start
  12.8 10.3 %collective-permute-start.1 = (bf16[128,1024]{1,0:T(8,128)(2,1)S(1)}, bf16[128,1024]{1,0:T(8,128)(2,1)S(1)}, u32[]{:S(2)}, u32[]{:S(2)}) collective-permute-start(bf16[128,1024]{1,0:T(8,128)(2,1)S(1)} %maximum_select_fusion.2), channel_id=1, source_target_pairs={{0,32},{16,48},{32,0},{48,16},{64,96},{80,112},{96,64},{112,80},{1... | collective-permute-start | bytes 786440 | tf_op jit(solution)/shard_map/ppermute | solution.py:13
  23.2 27.1 %collective-permute-start.2 = (bf16[256,1024]{1,0:T(8,128)(2,1)S(1)}, bf16[256,1024]{1,0:T(8,128)(2,1)S(1)}, u32[]{:S(2)}, u32[]{:S(2)}) collective-permute-start(bf16[256,1024]{1,0:T(8,128)(2,1)S(1)} %maximum_select_fusion.1), channel_id=1, source_target_pairs={{0,64},{16,80},{32,96},{48,112},{64,0},{80,16},{96,32},{112,48},{1... | collective-permute-start | bytes 1572872 | tf_op jit(solution)/shard_map/ppermute | solution.py:13
  50.8 53.9 %copy-start.2 = (bf16[2,1024,1024]{2,1,0:T(8,128)(2,1)S(1)}, bf16[2,1024,1024]{2,1,0:T(8,128)(2,1)}, u32[]{:S(2)}) copy-start(bf16[2,1024,1024]{2,1,0:T(8,128)(2,1)} %param.6) | copy-start | bytes 12582916
  50.8 51.0 %collective-permute-start.3 = (bf16[512,1024]{1,0:T(8,128)(2,1)S(1)}, bf16[512,1024]{1,0:T(8,128)(2,1)S(1)}, u32[]{:S(2)}, u32[]{:S(2)}) collective-permute-start(bf16[512,1024]{1,0:T(8,128)(2,1)S(1)} %maximum_select_fusion), channel_id=1, source_target_pairs={{0,128},{16,144},{32,160},{48,176},{64,192},{80,208},{96,224},{112... | collective-permute-start | bytes 3145736 | tf_op jit(solution)/shard_map/ppermute | solution.py:19
  107.3 219.7 %copy-start.1 = (bf16[32,1024]{1,0:T(8,128)(2,1)S(1)}, bf16[32,1024]{1,0:T(8,128)(2,1)}, u32[]{:S(2)}) copy-start(bf16[32,1024]{1,0:T(8,128)(2,1)} %param.7) | copy-start | bytes 196612
  107.3 305.7 %all-gather.2.cloned.1.call-start = ((), (), s32[]{:S(2)}) async-start(), calls=%async_computation.2 | async-start | bytes 1114112 | tf_op jit(solution)/shard_map/all_gather | solution.py:72
  418.1 46.5 %collective-permute-start.4 = (bf16[2,256,1024]{2,1,0:T(8,128)(2,1)S(1)}, bf16[2,256,1024]{2,1,0:T(8,128)(2,1)S(1)}, u32[]{:S(2)}, u32[]{:S(2)}) collective-permute-start(bf16[2,256,1024]{2,1,0:T(8,128)(2,1)S(1)} %select_convert_fusion), channel_id=1, source_target_pairs={{0,64},{16,80},{32,96},{48,112},{64,0},{80,16},{96,32},{112,48},{1... | collective-permute-start | bytes 3145736 | tf_op jit(solution)/shard_map/ppermute | solution.py:13
  465.4 15.7 %collective-permute-start.5 = (bf16[2,128,1024]{2,1,0:T(8,128)(2,1)S(1)}, bf16[2,128,1024]{2,1,0:T(8,128)(2,1)S(1)}, u32[]{:S(2)}, u32[]{:S(2)}) collective-permute-start(bf16[2,128,1024]{2,1,0:T(8,128)(2,1)S(1)} %select_convert_fusion.1), channel_id=1, source_target_pairs={{0,32},{16,48},{32,0},{48,16},{64,96},{80,112},{96,64},{112,80},{1... | collective-permute-start | bytes 1572872 | tf_op jit(solution)/shard_map/ppermute | solution.py:13
  481.4 3.4 collective-permute-start.6
  485.0 14.9 %collective-permute-start.7 = (bf16[64,1024]{1,0:T(8,128)(2,1)S(1)}, bf16[64,1024]{1,0:T(8,128)(2,1)S(1)}, u32[]{:S(2)}, u32[]{:S(2)}) collective-permute-start(bf16[64,1024]{1,0:T(8,128)(2,1)S(1)} %fusion.12), channel_id=1, source_target_pairs={{128,0},{144,16},{160,32},{176,48},{192,64},{208,80},{224,96},{240... | collective-permute-start | bytes 393224 | tf_op jit(solution)/shard_map/ppermute | solution.py:19
Sparse Core Ops, SparseCore 0:
  107.5 219.5 reduce-scatter.1
  330.8 82.2 all-gather.1
where the time goes:
time: 508 us
  waiting for transfers between devices  458 us (90%)
  starting transfers between devices  18.8 us (4%)
  between operations  14.4 us (3%)
  matrix products  10.3 us (2%)
  other arithmetic  5.64 us (1%)
    reduce_scatter x1, waiting for transfers between devices, local(): lax.psum_scatter(summed + jnp.dot(prior_all, decoders[1], preferred_eleme...  220 us
    ppermute x6, waiting for transfers between devices, swapped(): return lax.ppermute(value, axis, pairs)  92.6 us
    all_gather x1, waiting for transfers between devices, local(): lax.all_gather(errors_here, 'feat', axis=0, tiled=True)  84.4 us
    ppermute x2, waiting for transfers between devices, passed_along(): lax.ppermute(value, axis, [(source, source + steps) for source in range(f...  60.8 us
    ppermute x6, starting transfers between devices, swapped(): return lax.ppermute(value, axis, pairs)  13.6 us
  transfers between devices with their start and end apart: 10, of which 10 were waited for; matrix products, arithmetic and copies ran while one was open for 0% of the time, Pallas kernels for 0%

commit v1 on v0

--- a/solution.py
+++ b/solution.py
@@ -5,6 +5,13 @@
 
 D = 8192
 BLOCK = 128
+
+
+def exchange_gather(shard, name, along):
+    n_dev = lax.axis_size(name)
+    blocks = jnp.stack([shard for _ in range(n_dev)])
+    blocks = lax.all_to_all(blocks, name, split_axis=0, concat_axis=0)
+    return jnp.concatenate(blocks, axis=along)
 
 
 def swapped(value, axis, bit):
@@ -69,7 +76,7 @@
     errors_here = (recon_rows - targets.astype(jnp.float32)).astype(jnp.bfloat16)
     grad_terms = jnp.einsum(
         "tc,kfc->ktf",
-        lax.all_gather(errors_here, "feat", axis=0, tiled=True),
+        exchange_gather(errors_here, "feat", 0),
         decoders,
         preferred_element_type=jnp.float32,
     )

time: 508 us -> 449 us (0.88)
  waiting for transfers between devices: 458 us -> 370 us
  blocking collectives: 0 us -> 30.1 us
    all_gather x1 -> x0, waiting for transfers between devices: 84.4 us -> none  [local(): lax.all_gather(errors_here, 'feat', axis=0, tiled=True)]
    all_to_all x0 -> x1, blocking collectives: none -> 30.1 us  [exchange_gather(): blocks = lax.all_to_all(blocks, name, split_axis=0, concat_axis=0)]
  transfers between devices with their start and end apart: 10 -> 9, of which waited for: 10 -> 9; matrix products, arithmetic and copies ran while one was open for 0% -> 0% of each run, Pallas kernels for 0% -> 0%
where the time goes in v1:
time: 449 us
  waiting for transfers between devices  370 us (82%)
  blocking collectives  30.1 us (7%)
  starting transfers between devices  18.7 us (4%)
  between operations  14.4 us (3%)
  matrix products  10 us (2%)
  other arithmetic  5.01 us (1%)
    reduce_scatter x1, waiting for transfers between devices, local(): lax.psum_scatter(summed + jnp.dot(prior_all, decoders[1], preferred_eleme...  220 us
    ppermute x6, waiting for transfers between devices, swapped(): return lax.ppermute(value, axis, pairs)  89 us
    ppermute x2, waiting for transfers between devices, passed_along(): lax.ppermute(value, axis, [(source, source + steps) for source in range(f...  60.8 us
    all_to_all x1, blocking collectives, exchange_gather(): blocks = lax.all_to_all(blocks, name, split_axis=0, concat_axis=0)  30.1 us
    ppermute x6, starting transfers between devices, swapped(): return lax.ppermute(value, axis, pairs)  13.6 us
  transfers between devices with their start and end apart: 9, of which 9 were waited for; matrix products, arithmetic and copies ran while one was open for 0% of the time, Pallas kernels for 0%

profile of v1, /device:TPU:32, one launch (start us, length us, event | category | flops | bytes accessed | tf_op | source)
XLA Modules:
  0.0 448.8 jit_solution(7968806507836289974)
XLA Ops:
  7.3 0.7 copy-done
  7.9 0.4 compare_reduce_fusion
  8.4 0.1 broadcast_in_dim.15
  8.5 0.9 bitcast_select_fusion
  9.5 1.9 collective-permute-start
  11.4 1.3 collective-permute-done
  12.8 2.6 collective-permute-start.1
  15.4 7.6 %collective-permute-done.1 = bf16[128,1024]{1,0:T(8,128)(2,1)S(1)} collective-permute-done((bf16[128,1024]{1,0:T(8,128)(2,1)S(1)}, bf16[128,1024]{1,0:T(8,128)(2,1)S(1)}, u32[]{:S(2)}, u32[]{:S(2)}) %collective-permute-start.1) | collective-permute-done | bytes 262176 | tf_op jit(solution)/shard_map/ppermute | solution.py:20
  23.0 0.1 maximum_select_fusion.1
  23.2 2.7 collective-permute-start.2
  25.9 24.4 %collective-permute-done.2 = bf16[256,1024]{1,0:T(8,128)(2,1)S(1)} collective-permute-done((bf16[256,1024]{1,0:T(8,128)(2,1)S(1)}, bf16[256,1024]{1,0:T(8,128)(2,1)S(1)}, u32[]{:S(2)}, u32[]{:S(2)}) %collective-permute-start.2) | collective-permute-done | bytes 524320 | tf_op jit(solution)/shard_map/ppermute | solution.py:20
  50.3 0.5 maximum_select_fusion
  50.8 3.2 collective-permute-start.3
  54.0 47.8 %collective-permute-done.3 = bf16[512,1024]{1,0:T(8,128)(2,1)S(1)} collective-permute-done((bf16[512,1024]{1,0:T(8,128)(2,1)S(1)}, bf16[512,1024]{1,0:T(8,128)(2,1)S(1)}, u32[]{:S(2)}, u32[]{:S(2)}) %collective-permute-start.3) | collective-permute-done | bytes 1048608 | tf_op jit(solution)/shard_map/ppermute | solution.py:26
  101.9 2.9 fusion
  104.7 2.6 fusion.6
  107.4 219.7 %reduce-scatter.2.cloned.1.call-done = f32[32,1024]{1,0:T(8,128)} async-done(((f32[512,1024]{1,0:T(8,128)}), f32[32,1024]{1,0:T(8,128)}) %reduce-scatter.2.cloned.1.call-update) | async-done | bytes 131088 | tf_op jit(solution)/shard_map/reduce_scatter | solution.py:70
  327.0 0.9 subtract_convert_fusion
  328.1 30.1 %all_to_all.5 = bf16[16,32,1024]{2,1,0:T(8,128)(2,1)S(1)} all-to-all(bf16[16,32,1024]{2,1,0:T(8,128)(2,1)S(1)} %stack.2), channel_id=1, replica_groups=mesh['layer'=32,'feat'=16] {'feat'}, dimensions={0} | all-to-all | bytes 2097152 | tf_op jit(solution)/shard_map/all_to_all | solution.py:13
  358.2 4.6 %convolution_bitcast_fusion = f32[2,512,1024]{2,1,0:T(8,128)S(1)} fusion(bf16[512,1024,1]{1,0,2:T(8,128)(2,1)S(1)} %bitcast.32, bf16[2,1024,1024]{2,1,0:T(8,128)(2,1)} %param.6), kind=kOutput, calls=%fused_computation | convolution fusion | flops 2147483648 | bytes 9437184 | tf_op jit(solution)/shard_map/tc,kfc->ktf/dot_general | solution.py:77
  362.7 0.2 select_convert_fusion
  362.9 2.5 collective-permute-start.4
  365.5 40.4 %collective-permute-done.4 = bf16[2,256,1024]{2,1,0:T(8,128)(2,1)S(1)} collective-permute-done((bf16[2,256,1024]{2,1,0:T(8,128)(2,1)S(1)}, bf16[2,256,1024]{2,1,0:T(8,128)(2,1)S(1)}, u32[]{:S(2)}, u32[]{:S(2)}) %collective-permute-start.4) | collective-permute-done | bytes 1048608 | tf_op jit(solution)/shard_map/ppermute | solution.py:20
  405.9 0.6 convert_add_fusion
  406.6 1.9 collective-permute-start.5
  408.5 13.8 %collective-permute-done.5 = bf16[2,128,1024]{2,1,0:T(8,128)(2,1)S(1)} collective-permute-done((bf16[2,128,1024]{2,1,0:T(8,128)(2,1)S(1)}, bf16[2,128,1024]{2,1,0:T(8,128)(2,1)S(1)}, u32[]{:S(2)}, u32[]{:S(2)}) %collective-permute-start.5) | collective-permute-done | bytes 524320 | tf_op jit(solution)/shard_map/ppermute | solution.py:20
  422.3 0.3 convert_add_fusion.1
  422.6 1.9 collective-permute-start.6
  424.6 1.5 collective-permute-done.6
  426.2 1.9 collective-permute-start.7
  428.1 13.0 %collective-permute-done.7 = bf16[64,1024]{1,0:T(8,128)(2,1)S(1)} collective-permute-done((bf16[64,1024]{1,0:T(8,128)(2,1)S(1)}, bf16[64,1024]{1,0:T(8,128)(2,1)S(1)}, u32[]{:S(2)}, u32[]{:S(2)}) %collective-permute-start.7) | collective-permute-done | bytes 131104 | tf_op jit(solution)/shard_map/ppermute | solution.py:26
  441.2 0.8 fusion.10
  (19 shorter events, 0.6 us)
Async XLA Ops:
  7.2 0.8 copy-start
  7.2 319.8 %reduce-scatter.2.cloned.1.call-start = ((), (), s32[]{:S(2)}) async-start(), calls=%async_computation.2 | async-start | bytes 2228224 | tf_op jit(solution)/shard_map/reduce_scatter | solution.py:70
  9.5 3.2 collective-permute-start
  12.8 10.3 %collective-permute-start.1 = (bf16[128,1024]{1,0:T(8,128)(2,1)S(1)}, bf16[128,1024]{1,0:T(8,128)(2,1)S(1)}, u32[]{:S(2)}, u32[]{:S(2)}) collective-permute-start(bf16[128,1024]{1,0:T(8,128)(2,1)S(1)} %maximum_select_fusion.2), channel_id=1, source_target_pairs={{0,32},{16,48},{32,0},{48,16},{64,96},{80,112},{96,64},{112,80},{1... | collective-permute-start | bytes 786440 | tf_op jit(solution)/shard_map/ppermute | solution.py:20
  23.2 27.1 %collective-permute-start.2 = (bf16[256,1024]{1,0:T(8,128)(2,1)S(1)}, bf16[256,1024]{1,0:T(8,128)(2,1)S(1)}, u32[]{:S(2)}, u32[]{:S(2)}) collective-permute-start(bf16[256,1024]{1,0:T(8,128)(2,1)S(1)} %maximum_select_fusion.1), channel_id=1, source_target_pairs={{0,64},{16,80},{32,96},{48,112},{64,0},{80,16},{96,32},{112,48},{1... | collective-permute-start | bytes 1572872 | tf_op jit(solution)/shard_map/ppermute | solution.py:20
  50.8 53.9 %copy-start.3 = (bf16[2,1024,1024]{2,1,0:T(8,128)(2,1)S(1)}, bf16[2,1024,1024]{2,1,0:T(8,128)(2,1)}, u32[]{:S(2)}) copy-start(bf16[2,1024,1024]{2,1,0:T(8,128)(2,1)} %param.6) | copy-start | bytes 12582916
  50.8 51.0 %collective-permute-start.3 = (bf16[512,1024]{1,0:T(8,128)(2,1)S(1)}, bf16[512,1024]{1,0:T(8,128)(2,1)S(1)}, u32[]{:S(2)}, u32[]{:S(2)}) collective-permute-start(bf16[512,1024]{1,0:T(8,128)(2,1)S(1)} %maximum_select_fusion), channel_id=1, source_target_pairs={{0,128},{16,144},{32,160},{48,176},{64,192},{80,208},{96,224},{112... | collective-permute-start | bytes 3145736 | tf_op jit(solution)/shard_map/ppermute | solution.py:26
  107.3 219.7 %copy-start.2 = (bf16[32,1024]{1,0:T(8,128)(2,1)S(1)}, bf16[32,1024]{1,0:T(8,128)(2,1)}, u32[]{:S(2)}) copy-start(bf16[32,1024]{1,0:T(8,128)(2,1)} %param.7) | copy-start | bytes 196612
  327.9 34.8 %copy-start.1 = (bf16[32,1024]{1,0:T(8,128)(2,1)}, bf16[32,1024]{1,0:T(8,128)(2,1)S(1)}, u32[]{:S(2)}) copy-start(bf16[32,1024]{1,0:T(8,128)(2,1)S(1)} %subtract_convert_fusion) | copy-start | bytes 196612
  362.9 42.9 %collective-permute-start.4 = (bf16[2,256,1024]{2,1,0:T(8,128)(2,1)S(1)}, bf16[2,256,1024]{2,1,0:T(8,128)(2,1)S(1)}, u32[]{:S(2)}, u32[]{:S(2)}) collective-permute-start(bf16[2,256,1024]{2,1,0:T(8,128)(2,1)S(1)} %select_convert_fusion), channel_id=1, source_target_pairs={{0,64},{16,80},{32,96},{48,112},{64,0},{80,16},{96,32},{112,48},{1... | collective-permute-start | bytes 3145736 | tf_op jit(solution)/shard_map/ppermute | solution.py:20
  406.6 15.7 %collective-permute-start.5 = (bf16[2,128,1024]{2,1,0:T(8,128)(2,1)S(1)}, bf16[2,128,1024]{2,1,0:T(8,128)(2,1)S(1)}, u32[]{:S(2)}, u32[]{:S(2)}) collective-permute-start(bf16[2,128,1024]{2,1,0:T(8,128)(2,1)S(1)} %select_convert_fusion.1), channel_id=1, source_target_pairs={{0,32},{16,48},{32,0},{48,16},{64,96},{80,112},{96,64},{112,80},{1... | collective-permute-start | bytes 1572872 | tf_op jit(solution)/shard_map/ppermute | solution.py:20
  422.6 3.4 collective-permute-start.6
  426.2 14.9 %collective-permute-start.7 = (bf16[64,1024]{1,0:T(8,128)(2,1)S(1)}, bf16[64,1024]{1,0:T(8,128)(2,1)S(1)}, u32[]{:S(2)}, u32[]{:S(2)}) collective-permute-start(bf16[64,1024]{1,0:T(8,128)(2,1)S(1)} %fusion.11), channel_id=1, source_target_pairs={{128,0},{144,16},{160,32},{176,48},{192,64},{208,80},{224,96},{240... | collective-permute-start | bytes 393224 | tf_op jit(solution)/shard_map/ppermute | solution.py:26
Sparse Core Ops, SparseCore 0:
  107.5 219.5 reduce-scatter.1
